TPU v7x, 128 devices: a whole 4x4x4 slice. The times are simulated.
128 devices in a mesh: dp: 4 (over x), fsdp: 32 (over z, y, core).
Axes of the slice: x: 4, y: 4, z: 4, core: 2. Of those that a mesh axis runs over, the one named last changes fastest.
Arguments:
- mlp_input: bfloat16 [1024, 4096], P('dp', 'fsdp'), may hold values from -6 to 6
- residual_in: bfloat16 [1024, 4096], P(('dp', 'fsdp')), may hold values from -6 to 6
- gate_weight: bfloat16 [4096, 14336], P(None, 'fsdp'), may hold values from -0.09375 to 0.09375
- up_weight: bfloat16 [4096, 14336], P(None, 'fsdp'), may hold values from -0.09375 to 0.09375
- down_weight: bfloat16 [14336, 4096], P('fsdp'), may hold values from -0.046875 to 0.046875
- span_index: bfloat16 [65536, 4096], P(('dp', 'fsdp')), may hold values from -6 to 6
- positive_keys: bfloat16 [1024, 4096], P(('dp', 'fsdp')), may hold values from -6 to 6
- request_rows: int32 [128, 128, 8], P(None, ('dp', 'fsdp')), may hold values from 0 to 511, as said below
- request_counts: int32 [128, 128], P(None, ('dp', 'fsdp')), may hold values from 0 to 8, as said below
- negative_slots: int32 [1024, 64], P(('dp', 'fsdp')), may hold values from 0 to 1023, as said below
Outputs:
- query_loss: float32 [1024], P(('dp', 'fsdp'))
- input_grad: bfloat16 [1024, 4096], P('dp', 'fsdp')
- gate_grad: bfloat16 [4096, 14336], P('dp', 'fsdp')
- up_grad: bfloat16 [4096, 14336], P('dp', 'fsdp')
- down_grad: bfloat16 [14336, 4096], P('fsdp', 'dp')
Inputs may be any that keep to these rules, and one draw needn't show every extreme that they name: `request_rows`: entry [r, o, s] is a local row of shard o; it is read only where s < request_counts[r, o]. `request_counts`: for each requesting device r the counts over the 128 shards sum to 512, and some shard gets exactly 8. `negative_slots`: rows q of device r = q // 8; an entry o * 8 + s names slot s of shard o with s < request_counts[r, o]; the 512 entries of a device use each such slot exactly once.
All inputs are finite; a program needn't handle non-finite values.
Results may differ from a plain program's by a relative error of at most 0.017.
Values may be sent and summed in bfloat16 or wider, within the bound.
A program may use at most 128 MiB of HBM per device.

v0:
```python
import jax
import jax.numpy as jnp
from jax import lax
from jax.sharding import PartitionSpec as P

inverse_temp = 50.0
eps = 1e-06
contract_first = (((0,), (0,)), ((), ()))
contract_last = (((1,), (1,)), ((), ()))


def silu_grad(gate_act):
    sigmoid_gate = jax.nn.sigmoid(gate_act)
    return sigmoid_gate * (1.0 + gate_act * (1.0 - sigmoid_gate))


def contrast(unit_rows, row_norm, key_block):
    key_unit = key_block / jnp.sqrt(jnp.sum(key_block * key_block, axis=-1, keepdims=True) + eps)
    scores = inverse_temp * jnp.einsum(
        "qd,qnd->qn", unit_rows, key_unit, precision=lax.Precision.HIGHEST
    )
    weights = jnp.exp(scores)
    exp_total = jnp.sum(weights, axis=-1)
    query_loss = jnp.log(exp_total) - scores[:, 0]
    column = lax.broadcasted_iota(jnp.int32, scores.shape, 1)
    coeffs = weights / exp_total[:, None] - (column == 0).astype(scores.dtype)
    pull_term = inverse_temp * jnp.einsum(
        "qn,qnd->qd", coeffs, key_unit, precision=lax.Precision.HIGHEST
    )
    inner_term = jnp.sum(coeffs * scores, axis=-1)
    head_grad = ((pull_term - inner_term[:, None] * unit_rows) / row_norm[:, None]).astype(
        jnp.bfloat16
    )
    return (query_loss, head_grad)


def shards(
    mlp_input,
    residual_in,
    gate_weight,
    up_weight,
    down_weight,
    span_index,
    positive_keys,
    request_rows,
    request_counts,
    negative_slots,
):
    dp_count = lax.axis_size("dp")
    fsdp_count = lax.axis_size("fsdp")
    owners = dp_count * fsdp_count
    slot_cap = request_rows.shape[2]
    feature_width = span_index.shape[1]
    whole_input = lax.all_gather(mlp_input, "fsdp", axis=1, tiled=True)
    gate_act = jnp.dot(whole_input, gate_weight, preferred_element_type=jnp.float32)
    up_act = jnp.dot(whole_input, up_weight, preferred_element_type=jnp.float32)
    hidden = (jax.nn.silu(gate_act) * up_act).astype(jnp.bfloat16)
    branch = lax.psum_scatter(
        jnp.dot(hidden, down_weight, preferred_element_type=jnp.float32).astype(jnp.bfloat16),
        "fsdp",
        scatter_dimension=0,
        tiled=True,
    ).astype(jnp.float32)
    top_state = branch + residual_in.astype(jnp.float32)
    row_norm = jnp.sqrt(jnp.sum(top_state * top_state, axis=-1) + eps)
    unit_rows = top_state / row_norm[:, None]
    row_table = request_rows[:, 0, :]
    count_table = request_counts[:, 0]
    picked = jnp.take(span_index, row_table.reshape(-1), axis=0).reshape(
        owners, slot_cap, feature_width
    )
    live_mask = lax.broadcasted_iota(jnp.int32, (owners, slot_cap), 1) < count_table[:, None]
    picked = jnp.where(live_mask[..., None], picked, jnp.zeros_like(picked))
    buffer = lax.all_to_all(picked, ("dp", "fsdp"), split_axis=0, concat_axis=0, tiled=True)
    flat_buffer = buffer.reshape(owners * slot_cap, feature_width)
    fetched = jnp.take(flat_buffer, negative_slots.reshape(-1), axis=0)
    fetched = fetched.reshape(
        negative_slots.shape[0], negative_slots.shape[1], feature_width
    ).astype(jnp.float32)
    key_block = jnp.concatenate([positive_keys.astype(jnp.float32)[:, None, :], fetched], axis=1)
    query_loss, head_grad = contrast(unit_rows, row_norm, key_block)
    gathered_grad = lax.all_gather(head_grad, "fsdp", axis=0, tiled=True)
    hidden_grad = lax.dot_general(
        gathered_grad, down_weight, contract_last, preferred_element_type=jnp.float32
    )
    gate_grad_act = (hidden_grad * up_act * silu_grad(gate_act)).astype(jnp.bfloat16)
    up_grad_act = (hidden_grad * jax.nn.silu(gate_act)).astype(jnp.bfloat16)
    input_term = lax.dot_general(
        gate_grad_act, gate_weight, contract_last, preferred_element_type=jnp.float32
    ) + lax.dot_general(up_grad_act, up_weight, contract_last, preferred_element_type=jnp.float32)
    input_grad = lax.psum_scatter(
        input_term.astype(jnp.bfloat16), "fsdp", scatter_dimension=1, tiled=True
    )
    gate_term = lax.dot_general(
        whole_input, gate_grad_act, contract_first, preferred_element_type=jnp.float32
    )
    up_term = lax.dot_general(
        whole_input, up_grad_act, contract_first, preferred_element_type=jnp.float32
    )
    down_term = lax.dot_general(
        hidden, gathered_grad, contract_first, preferred_element_type=jnp.float32
    )
    gate_sum, up_sum = (
        lax.psum_scatter(
            gate_term.astype(jnp.bfloat16), "dp", scatter_dimension=0, tiled=True
        ).astype(jnp.float32),
        lax.psum_scatter(
            up_term.astype(jnp.bfloat16), "dp", scatter_dimension=0, tiled=True
        ).astype(jnp.float32),
    )
    down_sum = lax.psum_scatter(
        down_term.astype(jnp.bfloat16), "dp", scatter_dimension=1, tiled=True
    )
    gate_grad = gate_sum.astype(jnp.bfloat16)
    up_grad = up_sum.astype(jnp.bfloat16)
    return (query_loss, input_grad, gate_grad, up_grad, down_sum)


def solution(mesh):
    return jax.shard_map(
        shards,
        mesh=mesh,
        in_specs=(
            P("dp", "fsdp"),
            P(("dp", "fsdp"), None),
            P(None, "fsdp"),
            P(None, "fsdp"),
            P("fsdp", None),
            P(("dp", "fsdp"), None),
            P(("dp", "fsdp"), None),
            P(None, ("dp", "fsdp"), None),
            P(None, ("dp", "fsdp")),
            P(("dp", "fsdp"), None),
        ),
        out_specs=(
            P(("dp", "fsdp")),
            P("dp", "fsdp"),
            P("dp", "fsdp"),
            P("dp", "fsdp"),
            P("fsdp", "dp"),
        ),
        check_vma=False,
    )
```

profile of v0, /device:TPU:1, one launch (start us, length us, event | category | flops | bytes accessed | tf_op | source)
XLA Modules:
  0.0 547.2 jit_solution(9983815885430911765)
XLA Ops:
  10.4 17.8 %gather_fusion = bf16[1024,4096]{1,0:T(8,128)(2,1)} fusion(bf16[512,4096]{1,0:T(8,128)(2,1)} %param.15, s32[1024]{0:T(1024)S(1)} %broadcast_clamp_fusion), kind=kCustom, calls=%fused_computation | custom fusion | bytes 16781312 | tf_op jit(solution)/shard_map/jit(_take)/gather | solution.py:69
  28.2 7.4 %fusion.1 = bf16[128,8,4096]{2,1,0:T(8,128)(2,1)} fusion(bf16[1024,4096]{1,0:T(8,128)(2,1)} %gather_fusion, pred[128,8]{1,0:T(8,128)(4,1)S(1)} %copy.20, pred[128,8]{1,0:T(8,128)(4,1)S(1)} %iota_compare_fusion), kind=kLoop, calls=%fused_computation.6 | loop fusion | flops 8388608 | bytes 16779264 | tf_op jit(solution)/shard_map/jit(_where)/select_n | solution.py:73
  35.6 11.9 %all-to-all-start = ((bf16[128,8,4096]{2,1,0:T(8,128)(2,1)}), bf16[128,8,4096]{2,1,0:T(8,128)(2,1)}, u32[]{:S(2)}, u32[]{:S(2)}) async-start(bf16[128,8,4096]{2,1,0:T(8,128)(2,1)} %fusion.1), calls=%async_computation.1 | async-start | bytes 16777216 | tf_op jit(solution)/shard_map/all_to_all | solution.py:74
  47.6 94.3 %all-gather.3.cloned.1.call-done = bf16[256,4096]{1,0:T(8,128)(2,1)} async-done(((bf16[256,128]{1,0:T(8,128)(2,1)}), bf16[256,4096]{1,0:T(8,128)(2,1)}) %all-gather.3.cloned.1.call-update) | async-done | bytes 2097168 | tf_op jit(solution)/shard_map/all_gather | solution.py:54
  141.9 4.0 fusion.20
  146.3 1.9 multiply_convert_fusion.2
  148.4 2.6 convolution_convert_fusion.3
  151.5 80.2 %reduce-scatter.8.cloned.1.call-done = bf16[8,4096]{1,0:T(8,128)(2,1)} async-done(((bf16[256,4096]{1,0:T(8,128)(2,1)}), bf16[8,4096]{1,0:T(8,128)(2,1)}) %reduce-scatter.8.cloned.1.call-update) | async-done | bytes 65552 | tf_op jit(solution)/shard_map/reduce_scatter | solution.py:58
  233.6 13.1 %gather_fusion.1 = bf16[512,4096]{1,0:T(8,128)(2,1)} fusion(bf16[1024,4096]{1,0:T(8,128)(2,1)} %bitcast.6, s32[1024]{0:T(1024)S(1)} %pad_clamp_fusion), kind=kCustom, calls=%fused_computation.1 | custom fusion | bytes 8390656 | tf_op jit(solution)/shard_map/jit(_take)/gather | solution.py:76
  246.7 2.6 broadcast_select_fusion
  249.3 2.2 fusion
  251.5 8.5 %fusion.3 = f32[8,1,65]{2,1,0:T(1,128)S(1)} fusion(f32[8,65]{1,0:T(8,128)S(1)} %add_sqrt_fusion, bf16[8,64,4096]{2,1,0:T(8,128)(2,1)S(1)} %broadcast_select_fusion, bf16[8,1,4096]{2,1,0:T(2,128)(2,1)S(1)} %copy.22, f32[8,4096,1]{1,0,2:T(8,128)S(1)} %fusion.16), kind=kOutput, calls=%fused_computation.8 | convolution fusion | flops 36208640 | bytes 4395072 | tf_op jit(solution)/shard_map/qd,qnd->qn/dot_general | solution.py:19
  260.3 7.8 %fusion.2 = f32[8,1,4096]{2,1,0:T(1,128)S(1)} fusion(f32[8,65,1]{1,2,0:T(1,128)S(1)} %copy.25, f32[8,65]{1,0:T(8,128)S(1)} %add_sqrt_fusion, bf16[8,64,4096]{2,1,0:T(8,128)(2,1)} %copy-done, bf16[8,1,4096]{2,1,0:T(2,128)(2,1)S(1)} %copy.22), kind=kOutput, calls=%fused_computation.7 | convolution fusion | flops 36208640 | bytes 4395072 | tf_op jit(solution)/shard_map/qn,qnd->qd/dot_general | solution.py:27
  269.0 45.4 %all-gather.5.cloned.1.call-done = bf16[256,4096]{1,0:T(8,128)(2,1)} async-done(((bf16[8,4096]{1,0:T(8,128)(2,1)}), bf16[256,4096]{1,0:T(8,128)(2,1)}) %all-gather.5.cloned.1.call-update) | async-done | bytes 2097168 | tf_op jit(solution)/shard_map/all_gather | solution.py:82
  314.3 4.1 multiply_convert_fusion
  320.5 2.7 fusion.6
  323.2 4.1 copy.27
  327.4 2.9 fusion.4
  330.4 2.9 fusion.5
  334.9 3.0 convolution_convert_fusion
  338.5 65.1 %reduce-scatter.16.cloned.1.call-done = bf16[128,256]{1,0:T(8,128)(2,1)} async-done(((bf16[4096,256]{1,0:T(8,128)(2,1)}), bf16[128,256]{1,0:T(8,128)(2,1)}) %reduce-scatter.16.cloned.1.call-update) | async-done | bytes 65552
  405.2 44.7 %reduce-scatter.10.cloned.1.call-done = bf16[1024,448]{0,1:T(8,128)(2,1)} async-done(((bf16[4096,448]{0,1:T(8,128)(2,1)}), bf16[1024,448]{0,1:T(8,128)(2,1)}) %reduce-scatter.10.cloned.1.call-update) | async-done | bytes 917520 | tf_op jit(solution)/shard_map/reduce_scatter | solution.py:104
  449.9 45.1 %reduce-scatter.12.cloned.1.call-done = bf16[1024,448]{0,1:T(8,128)(2,1)} async-done(((bf16[4096,448]{0,1:T(8,128)(2,1)}), bf16[1024,448]{0,1:T(8,128)(2,1)}) %reduce-scatter.12.cloned.1.call-update) | async-done | bytes 917520 | tf_op jit(solution)/shard_map/reduce_scatter | solution.py:107
  495.1 45.3 %reduce-scatter.14.cloned.1.call-done = bf16[448,1024]{1,0:T(8,128)(2,1)} async-done(((bf16[448,4096]{1,0:T(8,128)(2,1)}), bf16[448,1024]{1,0:T(8,128)(2,1)}) %reduce-scatter.14.cloned.1.call-update) | async-done | bytes 917520 | tf_op jit(solution)/shard_map/reduce_scatter | solution.py:111
  (62 shorter events, 13.1 us)
Async XLA Ops:
  7.2 134.8 %all-gather.3.cloned.1.call-start = ((), (), s32[]{:S(2)}) async-start(), calls=%async_computation.6 | async-start | bytes 2162688 | tf_op jit(solution)/shard_map/all_gather | solution.py:54
  35.6 198.0 %all-to-all-start = ((bf16[128,8,4096]{2,1,0:T(8,128)(2,1)}), bf16[128,8,4096]{2,1,0:T(8,128)(2,1)}, u32[]{:S(2)}, u32[]{:S(2)}) async-start(bf16[128,8,4096]{2,1,0:T(8,128)(2,1)} %fusion.1), calls=%async_computation.1 | async-start | bytes 16777216 | tf_op jit(solution)/shard_map/all_to_all | solution.py:74
  47.6 184.1 %reduce-scatter.8.cloned.1.call-start = ((), (), s32[]{:S(2)}) async-start(), calls=%async_computation.7 | async-start | bytes 2162688 | tf_op jit(solution)/shard_map/reduce_scatter | solution.py:58
  141.9 4.0 copy-start.1
  141.9 4.4 copy-start.4
  146.3 2.0 copy-start.3
  148.3 3.0 copy-start.10
  148.3 3.1 copy-start.9
  148.3 83.4 %copy-start.7 = (bf16[8,4096]{1,0:T(8,128)(2,1)S(1)}, bf16[8,4096]{1,0:T(8,128)(2,1)}, u32[]{:S(2)}) copy-start(bf16[8,4096]{1,0:T(8,128)(2,1)} %param.11) | copy-start | bytes 196612
  151.0 163.3 %all-gather.5.cloned.1.call-start = ((), (), s32[]{:S(2)}) async-start(), calls=%async_computation.8 | async-start | bytes 2162688 | tf_op jit(solution)/shard_map/all_gather | solution.py:82
  249.3 2.2 copy-start
  260.3 7.8 %copy-start.8 = (bf16[8,4096]{1,0:T(8,128)(2,1)S(1)}, bf16[8,4096]{1,0:T(8,128)(2,1)}, u32[]{:S(2)}) copy-start(bf16[8,4096]{1,0:T(8,128)(2,1)} %reduce-scatter.8.cloned.1.call-done) | copy-start | bytes 196612
  268.9 134.7 %reduce-scatter.16.cloned.1.call-start = ((), (), s32[]{:S(2)}) async-start(), calls=%async_computation.12 | async-start | bytes 2162688
  314.3 4.1 copy-start.2
  318.4 2.0 copy-start.5
  327.3 122.6 %reduce-scatter.10.cloned.1.call-start = ((), (), s32[]{:S(2)}) async-start(), calls=%async_computation.9 | async-start | bytes 4587520 | tf_op jit(solution)/shard_map/reduce_scatter | solution.py:104
  330.3 164.7 %reduce-scatter.12.cloned.1.call-start = ((), (), s32[]{:S(2)}) async-start(), calls=%async_computation.10 | async-start | bytes 4587520 | tf_op jit(solution)/shard_map/reduce_scatter | solution.py:107
  333.3 1.6 copy-start.6
  333.3 207.0 %reduce-scatter.14.cloned.1.call-start = ((), (), s32[]{:S(2)}) async-start(), calls=%async_computation.11 | async-start | bytes 4587520 | tf_op jit(solution)/shard_map/reduce_scatter | solution.py:111
Sparse Core Ops, SparseCore 0:
  10.2 131.7 all-gather.2
  151.1 80.5 reduce-scatter.7
  269.1 45.2 all-gather.4
  327.4 76.1 reduce-scatter.15
  406.5 43.4 reduce-scatter.9
  452.8 42.2 reduce-scatter.11
  498.0 42.2 reduce-scatter.13
where the time goes:
time: 548 us; the launch traced here: 547 us
  waiting for transfers between devices  421 us (77%)
  matrix products  41.9 us (8%)
  local copies, waits for them, and re-layouts  40.7 us (7%)
  other arithmetic  17 us (3%)
  between operations  14.3 us (3%)
  starting transfers between devices  12.4 us (2%)
    all_gather x1, waiting for transfers between devices, shards(): whole_input = lax.all_gather(mlp_input, 'fsdp', axis=1, tiled=True)  94.3 us
    reduce_scatter x1, waiting for transfers between devices, shards(): lax.psum_scatter(jnp.dot(hidden, down_weight, preferred_element_type=jnp....  80.2 us
    unnamed x8, waiting for transfers between devices  65.9 us
    all_gather x1, waiting for transfers between devices, shards(): gathered_grad = lax.all_gather(head_grad, 'fsdp', axis=0, tiled=True)  45.4 us
    reduce_scatter x1, waiting for transfers between devices, shards(): lax.psum_scatter(down_term.astype(jnp.bfloat16), 'dp', scatter_dimension=...  45.3 us
    reduce_scatter x1, waiting for transfers between devices, shards(): lax.psum_scatter(up_term.astype(jnp.bfloat16), 'dp', scatter_dimension=0,...  45.1 us
    reduce_scatter x1, waiting for transfers between devices, shards(): lax.psum_scatter(gate_term.astype(jnp.bfloat16), 'dp', scatter_dimension=...  44.7 us
    gather x1, local copies, waits for them, and re-layouts, shards(): jnp.take(span_index, row_table.reshape(-1), axis=0)  17.8 us
  transfers between devices with their start and end apart: 8, of which 7 were waited for; matrix products, arithmetic and copies ran while one was open for 9% of the time, Pallas kernels for 0%

commit v1 on v0

--- a/solution.py
+++ b/solution.py
@@ -2,6 +2,7 @@
 import jax.numpy as jnp
 from jax import lax
 from jax.sharding import PartitionSpec as P
+from jax.lax import all_to_all, psum
 
 inverse_temp = 50.0
 eps = 1e-06
@@ -51,7 +52,9 @@
     owners = dp_count * fsdp_count
     slot_cap = request_rows.shape[2]
     feature_width = span_index.shape[1]
-    whole_input = lax.all_gather(mlp_input, "fsdp", axis=1, tiled=True)
+    whole_input = jnp.concatenate(
+        all_to_all(jnp.stack([mlp_input] * psum(1, "fsdp")), "fsdp", 0, 0), axis=1
+    )
     gate_act = jnp.dot(whole_input, gate_weight, preferred_element_type=jnp.float32)
     up_act = jnp.dot(whole_input, up_weight, preferred_element_type=jnp.float32)
     hidden = (jax.nn.silu(gate_act) * up_act).astype(jnp.bfloat16)

time: 548 us -> 496 us (0.905)
  waiting for transfers between devices: 421 us -> 364 us
    all_gather x1 -> x0, waiting for transfers between devices: 94.3 us -> none  [shards(): whole_input = lax.all_gather(mlp_input, 'fsdp', axis=1, tiled=True)]
    reduce_scatter x1, waiting for transfers between devices: 80.2 us -> 116 us  [shards(): lax.psum_scatter(jnp.dot(hidden, down_weight, preferred_element_type=jnp....]
    all_to_all x0 -> x1, starting transfers between devices: none -> 9.6 us  [shards(): all_to_all(jnp.stack([mlp_input] * psum(1, 'fsdp')), 'fsdp', 0, 0)]
    unnamed x8 -> x7, waiting for transfers between devices: 65.9 us -> 65.2 us
where the time goes in v1:
time: 496 us; the launch traced here: 495 us
  waiting for transfers between devices  364 us (73%)
  local copies, waits for them, and re-layouts  42.1 us (8%)
  matrix products  41.3 us (8%)
  starting transfers between devices  17.6 us (4%)
  other arithmetic  15.7 us (3%)
  between operations  14.4 us (3%)
    reduce_scatter x1, waiting for transfers between devices, shards(): lax.psum_scatter(jnp.dot(hidden, down_weight, preferred_element_type=jnp....  116 us
    unnamed x7, waiting for transfers between devices  65.2 us
    all_gather x1, waiting for transfers between devices, shards(): gathered_grad = lax.all_gather(head_grad, 'fsdp', axis=0, tiled=True)  45.3 us
    reduce_scatter x1, waiting for transfers between devices, shards(): lax.psum_scatter(down_term.astype(jnp.bfloat16), 'dp', scatter_dimension=...  45.1 us
    reduce_scatter x1, waiting for transfers between devices, shards(): lax.psum_scatter(up_term.astype(jnp.bfloat16), 'dp', scatter_dimension=0,...  45.1 us
    reduce_scatter x1, waiting for transfers between devices, shards(): lax.psum_scatter(gate_term.astype(jnp.bfloat16), 'dp', scatter_dimension=...  44.7 us
    gather x1, local copies, waits for them, and re-layouts, shards(): jnp.take(span_index, row_table.reshape(-1), axis=0)  17.8 us
    gather x1, local copies, waits for them, and re-layouts, shards(): fetched = jnp.take(flat_buffer, negative_slots.reshape(-1), axis=0)  13 us
  transfers between devices with their start and end apart: 8, of which 7 were waited for; matrix products, arithmetic and copies ran while one was open for 9% of the time, Pallas kernels for 0%

profile of v1, /device:TPU:1, one launch (start us, length us, event | category | flops | bytes accessed | tf_op | source)
XLA Modules:
  0.0 495.0 jit_solution(11528737958282596286)
XLA Ops:
  9.7 9.6 %all-to-all-start = ((bf16[32,256,128]{1,2,0:T(8,128)(2,1)}), bf16[32,256,128]{1,2,0:T(8,128)(2,1)S(1)}, u32[]{:S(2)}, u32[]{:S(2)}) async-start(bf16[32,256,128]{1,2,0:T(8,128)(2,1)} %stack.2), calls=%async_computation | async-start | bytes 4194304 | tf_op jit(solution)/shard_map/all_to_all | solution.py:56
  19.7 17.8 %gather_fusion = bf16[1024,4096]{1,0:T(8,128)(2,1)} fusion(bf16[512,4096]{1,0:T(8,128)(2,1)} %param.15, s32[1024]{0:T(1024)S(1)} %broadcast_clamp_fusion), kind=kCustom, calls=%fused_computation | custom fusion | bytes 16781312 | tf_op jit(solution)/shard_map/jit(_take)/gather | solution.py:72
  37.6 7.4 %fusion.1 = bf16[128,8,4096]{2,1,0:T(8,128)(2,1)} fusion(bf16[1024,4096]{1,0:T(8,128)(2,1)} %gather_fusion, pred[128,8]{1,0:T(8,128)(4,1)S(1)} %copy.22, pred[128,8]{1,0:T(8,128)(4,1)S(1)} %iota_compare_fusion), kind=kLoop, calls=%fused_computation.6 | loop fusion | flops 8388608 | bytes 16779264 | tf_op jit(solution)/shard_map/jit(_where)/select_n | solution.py:76
  45.0 2.1 all-to-all-done
  47.1 7.6 %all-to-all-start.1 = ((bf16[128,8,4096]{2,1,0:T(8,128)(2,1)}), bf16[128,8,4096]{2,1,0:T(8,128)(2,1)}, u32[]{:S(2)}, u32[]{:S(2)}) async-start(bf16[128,8,4096]{2,1,0:T(8,128)(2,1)} %fusion.1), calls=%async_computation.2 | async-start | bytes 16777216 | tf_op jit(solution)/shard_map/all_to_all | solution.py:77
  54.8 3.3 fusion.21
  60.2 2.6 convolution_convert_fusion.3
  63.3 116.4 %reduce-scatter.8.cloned.1.call-done = bf16[8,4096]{1,0:T(8,128)(2,1)} async-done(((bf16[256,4096]{1,0:T(8,128)(2,1)}), bf16[8,4096]{1,0:T(8,128)(2,1)}) %reduce-scatter.8.cloned.1.call-update) | async-done | bytes 65552 | tf_op jit(solution)/shard_map/reduce_scatter | solution.py:61
  181.6 13.0 %gather_fusion.1 = bf16[512,4096]{1,0:T(8,128)(2,1)} fusion(bf16[1024,4096]{1,0:T(8,128)(2,1)} %bitcast.9, s32[1024]{0:T(1024)S(1)} %pad_clamp_fusion), kind=kCustom, calls=%fused_computation.1 | custom fusion | bytes 8390656 | tf_op jit(solution)/shard_map/jit(_take)/gather | solution.py:79
  194.7 2.6 broadcast_select_fusion
  197.3 2.2 fusion
  199.5 8.5 %fusion.3 = f32[8,1,65]{2,1,0:T(1,128)S(1)} fusion(f32[8,65]{1,0:T(8,128)S(1)} %add_sqrt_fusion, bf16[8,64,4096]{2,1,0:T(8,128)(2,1)S(1)} %broadcast_select_fusion, bf16[8,1,4096]{2,1,0:T(2,128)(2,1)S(1)} %copy.24, f32[8,4096,1]{1,0,2:T(8,128)S(1)} %fusion.16), kind=kOutput, calls=%fused_computation.8 | convolution fusion | flops 36208640 | bytes 4395072 | tf_op jit(solution)/shard_map/qd,qnd->qn/dot_general | solution.py:20
  208.3 7.8 %fusion.2 = f32[8,1,4096]{2,1,0:T(1,128)S(1)} fusion(f32[8,65,1]{1,2,0:T(1,128)S(1)} %copy.27, f32[8,65]{1,0:T(8,128)S(1)} %add_sqrt_fusion, bf16[8,64,4096]{2,1,0:T(8,128)(2,1)} %copy-done, bf16[8,1,4096]{2,1,0:T(2,128)(2,1)S(1)} %copy.24), kind=kOutput, calls=%fused_computation.7 | convolution fusion | flops 36208640 | bytes 4395072 | tf_op jit(solution)/shard_map/qn,qnd->qd/dot_general | solution.py:28
  217.0 45.3 %all-gather.2.cloned.1.call-done = bf16[256,4096]{1,0:T(8,128)(2,1)} async-done(((bf16[8,4096]{1,0:T(8,128)(2,1)}), bf16[256,4096]{1,0:T(8,128)(2,1)}) %all-gather.2.cloned.1.call-update) | async-done | bytes 2097168 | tf_op jit(solution)/shard_map/all_gather | solution.py:85
  262.3 4.1 multiply_convert_fusion
  268.5 2.7 fusion.6
  271.2 4.1 copy.29
  275.3 3.0 fusion.4
  278.4 3.0 fusion.5
  283.0 3.0 convolution_convert_fusion
  286.6 65.1 %reduce-scatter.16.cloned.1.call-done = bf16[128,256]{1,0:T(8,128)(2,1)} async-done(((bf16[4096,256]{1,0:T(8,128)(2,1)}), bf16[128,256]{1,0:T(8,128)(2,1)}) %reduce-scatter.16.cloned.1.call-update) | async-done | bytes 65552
  353.2 44.7 %reduce-scatter.10.cloned.1.call-done = bf16[1024,448]{0,1:T(8,128)(2,1)} async-done(((bf16[4096,448]{0,1:T(8,128)(2,1)}), bf16[1024,448]{0,1:T(8,128)(2,1)}) %reduce-scatter.10.cloned.1.call-update) | async-done | bytes 917520 | tf_op jit(solution)/shard_map/reduce_scatter | solution.py:107
  397.9 45.1 %reduce-scatter.12.cloned.1.call-done = bf16[1024,448]{0,1:T(8,128)(2,1)} async-done(((bf16[4096,448]{0,1:T(8,128)(2,1)}), bf16[1024,448]{0,1:T(8,128)(2,1)}) %reduce-scatter.12.cloned.1.call-update) | async-done | bytes 917520 | tf_op jit(solution)/shard_map/reduce_scatter | solution.py:110
  443.0 45.1 %reduce-scatter.14.cloned.1.call-done = bf16[448,1024]{1,0:T(8,128)(2,1)} async-done(((bf16[448,4096]{1,0:T(8,128)(2,1)}), bf16[448,1024]{1,0:T(8,128)(2,1)}) %reduce-scatter.14.cloned.1.call-update) | async-done | bytes 917520 | tf_op jit(solution)/shard_map/reduce_scatter | solution.py:114
  (65 shorter events, 14.4 us)
Async XLA Ops:
  7.2 12.1 %copy-start.9 = (s32[128,1,8]{0,2,1:T(8,128)S(1)}, s32[128,1,8]{0,2,1:T(8,128)}, u32[]{:S(2)}) copy-start(s32[128,1,8]{0,2,1:T(8,128)} %param.17) | copy-start | bytes 12292
  9.7 37.5 %all-to-all-start = ((bf16[32,256,128]{1,2,0:T(8,128)(2,1)}), bf16[32,256,128]{1,2,0:T(8,128)(2,1)S(1)}, u32[]{:S(2)}, u32[]{:S(2)}) async-start(bf16[32,256,128]{1,2,0:T(8,128)(2,1)} %stack.2), calls=%async_computation | async-start | bytes 4194304 | tf_op jit(solution)/shard_map/all_to_all | solution.py:56
  19.7 17.8 %copy-start.11 = (s32[128,1]{0,1:T(1,128)S(1)}, s32[128,1]{0,1:T(1,128)}, u32[]{:S(2)}) copy-start(s32[128,1]{0,1:T(1,128)} %param.18) | copy-start | bytes 1540
  47.1 134.5 %all-to-all-start.1 = ((bf16[128,8,4096]{2,1,0:T(8,128)(2,1)}), bf16[128,8,4096]{2,1,0:T(8,128)(2,1)}, u32[]{:S(2)}, u32[]{:S(2)}) async-start(bf16[128,8,4096]{2,1,0:T(8,128)(2,1)} %fusion.1), calls=%async_computation.2 | async-start | bytes 16777216 | tf_op jit(solution)/shard_map/all_to_all | solution.py:77
  54.8 124.9 %reduce-scatter.8.cloned.1.call-start = ((), (), s32[]{:S(2)}) async-start(), calls=%async_computation.7 | async-start | bytes 2162688 | tf_op jit(solution)/shard_map/reduce_scatter | solution.py:61
  54.8 3.3 copy-start.3
  58.1 2.0 copy-start.2
  60.1 3.0 copy-start.10
  60.1 3.1 copy-start.8
  60.1 119.6 %copy-start.6 = (bf16[8,4096]{1,0:T(8,128)(2,1)S(1)}, bf16[8,4096]{1,0:T(8,128)(2,1)}, u32[]{:S(2)}) copy-start(bf16[8,4096]{1,0:T(8,128)(2,1)} %param.11) | copy-start | bytes 196612
  62.8 199.5 %all-gather.2.cloned.1.call-start = ((), (), s32[]{:S(2)}) async-start(), calls=%async_computation.8 | async-start | bytes 2162688 | tf_op jit(solution)/shard_map/all_gather | solution.py:85
  197.3 2.2 copy-start
  208.3 7.8 %copy-start.7 = (bf16[8,4096]{1,0:T(8,128)(2,1)S(1)}, bf16[8,4096]{1,0:T(8,128)(2,1)}, u32[]{:S(2)}) copy-start(bf16[8,4096]{1,0:T(8,128)(2,1)} %reduce-scatter.8.cloned.1.call-done) | copy-start | bytes 196612
  216.9 134.7 %reduce-scatter.16.cloned.1.call-start = ((), (), s32[]{:S(2)}) async-start(), calls=%async_computation.12 | async-start | bytes 2162688
  262.3 4.1 copy-start.1
  266.4 2.0 copy-start.4
  275.3 122.6 %reduce-scatter.10.cloned.1.call-start = ((), (), s32[]{:S(2)}) async-start(), calls=%async_computation.9 | async-start | bytes 4587520 | tf_op jit(solution)/shard_map/reduce_scatter | solution.py:107
  278.3 164.7 %reduce-scatter.12.cloned.1.call-start = ((), (), s32[]{:S(2)}) async-start(), calls=%async_computation.10 | async-start | bytes 4587520 | tf_op jit(solution)/shard_map/reduce_scatter | solution.py:110
  281.3 1.6 copy-start.5
  281.4 206.8 %reduce-scatter.14.cloned.1.call-start = ((), (), s32[]{:S(2)}) async-start(), calls=%async_computation.11 | async-start | bytes 4587520 | tf_op jit(solution)/shard_map/reduce_scatter | solution.py:114
Sparse Core Ops, SparseCore 0:
  63.0 116.6 reduce-scatter.7
  217.0 45.2 all-gather.1
  275.4 76.1 reduce-scatter.15
  354.5 43.3 reduce-scatter.9
  400.7 42.2 reduce-scatter.11
  445.8 42.2 reduce-scatter.13
